TPU v7x, 512 devices: a whole 4x8x8 slice. The times are simulated.
512 devices in a mesh: sub: 16 (over z, core), tile: 32 (over y, x).
Axes of the slice: x: 4, y: 8, z: 8, core: 2. Of those that a mesh axis runs over, the one named last changes fastest.
Arguments:
- echoes: float32 [32, 32, 128], P('sub', 'tile'), may hold values from -6 to 6
- pulse_offset: float32 [32, 32], P('sub', 'tile'), may hold values from 0 to 1
- range_gates: int32 [32, 32, 64], P('sub', 'tile'), may hold values from 0 to 511
- visible: int32 [32, 256], P('sub', 'tile'), may hold values 0 or 1
Outputs:
- images: float32 [32, 256, 128, 256], P('sub', 'tile')
- peak: float32 [256, 128, 128], P('tile', 'sub')
All inputs are finite; a program needn't handle non-finite values. No bound on the sum of `visible` on one device may be relied on, other than what follows from the above.
Results may differ from a plain program's by a relative error of at most 0.0037.
Values sent between devices are 32-bit elements; how exact they have to be, the bound alone decides.
No kernel may reach another device: no remote copies, remote signals or barrier semaphores. Data moves between devices by JAX's collectives and lax.ppermute only.
A program may use at most 64 MiB of HBM per device.

v0:
```python
import math
import jax
import jax.numpy as jnp
from jax import lax
from jax.sharding import PartitionSpec as P

PULSE_H = 32
FREQS = 64
PIX = 128
GATES = 512
grid_cols = 16
two_pi = 2.0 * math.pi


def shifted(block, axis, distance):
    devices = range(lax.axis_size(axis))
    route = [((i - distance) % len(devices), i) for i in devices]
    return lax.ppermute(block, axis, route)


def make_right(sine_wave):
    pixels = jnp.arange(PIX, dtype=jnp.float32)
    phase_grid = sine_wave[:, None] * pixels[None, :]
    real_part = jnp.cos(phase_grid).astype(jnp.bfloat16)
    imag_part = jnp.sin(phase_grid).astype(jnp.bfloat16)
    upper = jnp.concatenate([real_part, imag_part], axis=1)
    lower = jnp.concatenate([-imag_part, real_part], axis=1)
    return jnp.concatenate([upper, lower], axis=0)


def make_base(cosine_wave):
    pixels = jnp.arange(PIX, dtype=jnp.float32)
    base_phase = cosine_wave[None, :] * pixels[:, None]
    return (jnp.cos(base_phase), jnp.sin(base_phase))


def make_left(
    echo_real, echo_imag, cosine_wave, sine_wave, base_cos, base_sin, tile_number, norm_scale
):
    column = (tile_number % grid_cols * PIX - 8 * PIX).astype(jnp.float32)
    row_start = (tile_number // grid_cols * PIX - 4 * PIX).astype(jnp.float32)
    offset_phase = cosine_wave * column + sine_wave * row_start
    offset_cos = jnp.cos(offset_phase)
    offset_sin = jnp.sin(offset_phase)
    turned_real = norm_scale * (echo_real * offset_cos - echo_imag * offset_sin)
    turned_imag = norm_scale * (echo_real * offset_sin + echo_imag * offset_cos)
    real_part = turned_real[None, :] * base_cos - turned_imag[None, :] * base_sin
    imag_part = turned_real[None, :] * base_sin + turned_imag[None, :] * base_cos
    return jnp.concatenate([real_part, imag_part], axis=1).astype(jnp.bfloat16)


def on_device(echoes, pulse_offset, range_gates, visible):
    half_dev = echoes.shape[0]
    tile_dev = visible.shape[1]
    sub_count = lax.axis_size("sub")
    half_total = half_dev * sub_count
    first_half = lax.axis_index("sub") * half_dev
    first_tile = lax.axis_index("tile") * tile_dev
    half_numbers = first_half + jnp.arange(half_dev, dtype=jnp.int32)
    angles = two_pi * (half_numbers.astype(jnp.float32)[:, None] + pulse_offset) / half_total
    waves = 0.5 + range_gates.astype(jnp.float32) / GATES
    shown = visible.astype(jnp.float32)
    half_count = echoes.shape[0]
    norm_scale = (2.0 * PULSE_H * FREQS) ** (-0.5)
    echo_piece = lax.all_gather(echoes, "tile", axis=1, tiled=True)
    wave_piece = lax.all_gather(waves, "tile", axis=1, tiled=True)
    angle_piece = lax.all_gather(angles, "tile", axis=1, tiled=True)
    stacked = []
    for half_slot in range(half_count):
        cosine_wave = (wave_piece[half_slot] * jnp.cos(angle_piece[half_slot])[:, None]).reshape(-1)
        sine_wave = (wave_piece[half_slot] * jnp.sin(angle_piece[half_slot])[:, None]).reshape(-1)
        echo_real = echo_piece[half_slot][:, :FREQS].reshape(-1)
        echo_imag = echo_piece[half_slot][:, FREQS:].reshape(-1)
        right_side = make_right(sine_wave)
        base_cos, base_sin = make_base(cosine_wave)
        tile_terms = []
        for tile_slot in range(tile_dev):

            def compute(
                echo_real=echo_real,
                echo_imag=echo_imag,
                cosine_wave=cosine_wave,
                sine_wave=sine_wave,
                base_cos=base_cos,
                base_sin=base_sin,
                right_side=right_side,
                tile_slot=tile_slot,
            ):
                left_side = make_left(
                    echo_real,
                    echo_imag,
                    cosine_wave,
                    sine_wave,
                    base_cos,
                    base_sin,
                    first_tile + tile_slot,
                    norm_scale,
                )
                return jnp.dot(left_side, right_side, preferred_element_type=jnp.float32)

            tile_term = compute()
            tile_terms.append(tile_term)
        stacked.append(jnp.stack(tile_terms))
    half_images = jnp.stack(stacked)
    half_images = half_images * shown[:, :, None, None]
    following = shifted(half_images[0], "sub", -1)
    successors = jnp.concatenate([half_images[1:half_dev], following[None]], axis=0)
    images = half_images + successors
    power_map = images[..., :PIX] ** 2 + images[..., PIX:] ** 2
    local_peak = jnp.max(power_map, axis=0)
    full_peak = lax.pmax(local_peak, "sub")
    row_count = PIX // sub_count
    peak = lax.dynamic_slice_in_dim(full_peak, lax.axis_index("sub") * row_count, row_count, 1)
    return (images, peak)


def solution(mesh):
    in_specs = (P("sub", "tile", None), P("sub", "tile"), P("sub", "tile", None), P("sub", "tile"))
    out_specs = (P("sub", "tile", None, None), P("tile", "sub", None))
    return jax.shard_map(
        on_device, mesh=mesh, in_specs=in_specs, out_specs=out_specs, check_vma=False
    )
```

profile of v0, /device:TPU:1, one launch (start us, length us, event | category | flops | bytes accessed | tf_op | source)
XLA Modules:
  0.0 301.1 jit_solution(487523907034118992)
XLA Ops:
  7.2 0.0 all-reduce.2.cloned.1.call-start
  7.3 0.7 multiply_bitcast_fusion
  8.0 29.8 %all-gather = f32[32,1,2]{2,1,0:T(1,128)S(1)} all-gather(f32[1,1,2]{2,1,0:T(1,128)S(1)} %multiply_bitcast_fusion), channel_id=1, replica_groups=mesh['sub'=16,'tile'=32] {'tile'}, dimensions={0}, use_global_device_ids=true | all-gather | bytes 264 | tf_op jit(solution)/shard_map/all_gather | solution.py:67
  37.8 0.1 copy.9
  37.9 0.1 sine_bitcast_fusion.1
  37.9 0.1 mul.1893
  38.0 0.1 mul.1894
  38.1 0.1 mul.1900
  38.1 0.1 mul.1901
  38.2 0.1 mul.2050
  38.3 0.1 mul.2051
  38.3 0.1 mul.2054
  38.4 0.1 mul.2055
  38.5 29.0 %all_gather.9 = f32[2,32,128]{2,0,1:T(2,128)S(1)} all-gather(f32[2,1,128]{2,0,1:T(2,128)} %bitcast.94), channel_id=1, replica_groups=mesh['sub'=16,'tile'=32] {'tile'}, dimensions={1}, use_global_device_ids=true | all-gather | bytes 33792 | tf_op jit(solution)/shard_map/all_gather | solution.py:65
  67.5 0.1 fusion.122
  67.6 0.1 reshape.961
  67.6 0.1 reshape.962
  67.7 0.1 fusion.123
  67.8 0.1 reshape.963
  67.9 0.1 reshape.964
  67.9 0.7 multiply_add_fusion.16
  68.6 28.6 %all_gather.10 = f32[2,32,64]{2,0,1:T(2,128)S(1)} all-gather(f32[2,1,64]{2,0,1:T(2,128)S(1)} %multiply_add_fusion.16), channel_id=1, replica_groups=mesh['sub'=16,'tile'=32] {'tile'}, dimensions={1}, use_global_device_ids=true | all-gather | bytes 16896 | tf_op jit(solution)/shard_map/all_gather | solution.py:66
  97.2 0.1 slice_reduce_fusion.1
  97.3 0.1 squeeze.11
  97.4 0.1 squeeze.26
  97.4 0.1 subtract_multiply_fusion
  97.5 4.5 %sine_convert_fusion.1 = (bf16[2048,128]{1,0:T(8,128)(2,1)S(1)}, bf16[2048,128]{1,0:T(8,128)(2,1)S(1)}) fusion(f32[2048]{0:T(1024)S(1)} %get-tuple-element.117), kind=kLoop, calls=%fused_computation.125 | loop fusion | flops 786432 | bytes 1056768 | tf_op jit(solution)/shard_map/convert_element_type | solution.py:25
  102.0 4.1 %fusion.70 = bf16[2048,128]{1,0:T(8,128)(2,1)S(1)} fusion(f32[2048]{0:T(1024)S(1)} %get-tuple-element.117), kind=kLoop, calls=%fused_computation.133 | loop fusion | flops 1310720 | bytes 532480 | tf_op jit(solution)/shard_map/neg | solution.py:27
  106.2 0.1 subtract_multiply_fusion.15
  106.2 0.1 subtract_multiply_fusion.7
  106.3 0.3 add_multiply_fusion.8
  106.6 0.3 add_multiply_fusion
  106.8 4.5 %sine_convert_fusion = (bf16[2048,128]{1,0:T(8,128)(2,1)S(1)}, bf16[2048,128]{1,0:T(8,128)(2,1)S(1)}) fusion(f32[2048]{0:T(1024)S(1)} %get-tuple-element.9), kind=kLoop, calls=%fused_computation.103 | loop fusion | flops 786432 | bytes 1056768 | tf_op jit(solution)/shard_map/convert_element_type | solution.py:25
  111.3 4.1 %fusion.71 = bf16[2048,128]{1,0:T(8,128)(2,1)S(1)} fusion(f32[2048]{0:T(1024)S(1)} %get-tuple-element.9), kind=kLoop, calls=%fused_computation.134 | loop fusion | flops 1310720 | bytes 532480 | tf_op jit(solution)/shard_map/neg | solution.py:27
  115.4 0.0 copy-done.1
  115.4 6.3 %subtract_convert_fusion.8 = (bf16[128,2048]{1,0:T(8,128)(2,1)S(1)}, bf16[128,2048]{1,0:T(8,128)(2,1)S(1)}, bf16[128,2048]{1,0:T(8,128)(2,1)S(1)}, bf16[128,2048...) fusion(f32[2048]{0:T(1024)S(1)} %get-tuple-element.12, ...), kind=kLoop, calls=%fused_computation.112 | loop fusion | flops 17039360 | bytes 8527872 | tf_op jit(solution)/shard_map/convert.16
  121.7 0.5 fusion.15
  122.2 0.5 fusion.14
  122.6 0.5 fusion.13
  123.1 0.5 fusion.12
  123.6 0.5 fusion.11
  124.1 0.5 fusion.10
  124.6 0.5 fusion.9
  125.1 0.5 fusion.8
  125.6 6.2 %subtract_convert_fusion = (bf16[128,2048]{1,0:T(8,128)(2,1)S(1)}, bf16[128,2048]{1,0:T(8,128)(2,1)S(1)}, bf16[128,2048]{1,0:T(8,128)(2,1)S(1)}, bf16[128,2048]{...) fusion(f32[2048]{0:T(1024)S(1)} %get-tuple-element.29, ...), kind=kLoop, calls=%fused_computation.90 | loop fusion | flops 17039360 | bytes 8527872 | tf_op jit(solution)/shard_map/convert
  131.8 0.4 fusion.7
  132.2 0.4 fusion.6
  132.7 0.4 fusion.5
  133.1 0.4 fusion.4
  133.6 0.4 fusion.3
  134.0 0.5 fusion.2
  134.5 0.5 fusion.1
  135.0 0.5 fusion
  135.5 0.3 maximum_multiply_fusion
  135.7 0.2 fusion.120
  135.9 25.8 %collective-permute-start = (f32[8,128,256]{2,1,0:T(8,128)S(1)}, f32[8,128,256]{2,1,0:T(8,128)S(1)}, u32[]{:S(2)}, u32[]{:S(2)}) collective-permute-start(f32[8,128,256]{2,1,0:T(8,128)S(1)} %get-tuple-element.11), channel_id=1, source_target_pairs={{32,0},{64,32},{96,64},{128,96},{160,128},{192,160},{224,192},{256... | collective-permute-start | bytes 3145736 | tf_op jit(solution)/shard_map/ppermute | solution.py:18
  161.7 13.5 %collective-permute-done = f32[8,128,256]{2,1,0:T(8,128)S(1)} collective-permute-done((f32[8,128,256]{2,1,0:T(8,128)S(1)}, f32[8,128,256]{2,1,0:T(8,128)S(1)}, u32[]{:S(2)}, u32[]{:S(2)}) %collective-permute-start) | collective-permute-done | bytes 1048608 | tf_op jit(solution)/shard_map/ppermute | solution.py:18
  175.2 0.3 maximum_add_fusion
  175.6 0.0 copy-start
  175.6 1.1 fusion.17
  176.7 0.0 all-reduce.2.cloned.1.call-update
  176.7 116.2 %all-reduce.2.cloned.1.call-done = f32[8,128,128]{2,1,0:T(8,128)} async-done(((f32[8,128,128]{2,1,0:T(8,128)}), f32[8,128,128]{2,1,0:T(8,128)}) %all-reduce.2.cloned.1.call-update) | async-done | bytes 524304 | tf_op jit(solution)/shard_map/pmax | solution.py:111
  292.9 1.4 constant_dynamic-slice_fusion
  294.3 0.0 copy-done
  (3 shorter events, 0.0 us)
Async XLA Ops:
  7.2 285.7 %all-reduce.2.cloned.1.call-start = ((), (), s32[]{:S(2)}) async-start(), calls=%async_computation | async-start | bytes 1048576 | tf_op jit(solution)/shard_map/pmax | solution.py:111
  67.7 47.7 %copy-start.1 = (s32[2,8]{1,0:T(2,128)S(1)}, s32[2,8]{1,0:T(2,128)}, u32[]{:S(2)}) copy-start(s32[2,8]{1,0:T(2,128)} %param.7) | copy-start | bytes 196
  135.9 39.3 %collective-permute-start = (f32[8,128,256]{2,1,0:T(8,128)S(1)}, f32[8,128,256]{2,1,0:T(8,128)S(1)}, u32[]{:S(2)}, u32[]{:S(2)}) collective-permute-start(f32[8,128,256]{2,1,0:T(8,128)S(1)} %get-tuple-element.11), channel_id=1, source_target_pairs={{32,0},{64,32},{96,64},{128,96},{160,128},{192,160},{224,192},{256... | collective-permute-start | bytes 3145736 | tf_op jit(solution)/shard_map/ppermute | solution.py:18
  175.6 118.7 %copy-start = (f32[2,8,128,256]{3,2,1,0:T(8,128)}, f32[2,8,128,256]{3,2,1,0:T(8,128)S(1)}, u32[]{:S(2)}) copy-start(f32[2,8,128,256]{3,2,1,0:T(8,128)S(1)} %maximum_add_fusion) | copy-start | bytes 6291460
Sparse Core Ops, SparseCore 0:
  176.8 116.0 all-reduce.1
where the time goes:
time: 301 us
  waiting for transfers between devices  130 us (43%)
  blocking collectives  87.4 us (29%)
  other arithmetic  33.3 us (11%)
  starting transfers between devices  25.8 us (9%)
  between operations  14.5 us (5%)
  matrix products  7.47 us (2%)
    pmax x1, waiting for transfers between devices, on_device(): full_peak = lax.pmax(local_peak, 'sub')  116 us
    all_gather x1, blocking collectives, on_device(): angle_piece = lax.all_gather(angles, 'tile', axis=1, tiled=True)  29.8 us
    all_gather x1, blocking collectives, on_device(): echo_piece = lax.all_gather(echoes, 'tile', axis=1, tiled=True)  29 us
    all_gather x1, blocking collectives, on_device(): wave_piece = lax.all_gather(waves, 'tile', axis=1, tiled=True)  28.6 us
    ppermute x1, starting transfers between devices, shifted(): return lax.ppermute(block, axis, route)  25.8 us
    ppermute x1, waiting for transfers between devices, shifted(): return lax.ppermute(block, axis, route)  13.5 us
    another operation x2, other arithmetic  12.5 us
    convert_element_type x2, other arithmetic, make_right(): imag_part = jnp.sin(phase_grid).astype(jnp.bfloat16)  8.92 us
  transfers between devices with their start and end apart: 2, of which 2 were waited for; matrix products, arithmetic and copies ran while one was open for 0% of the time, Pallas kernels for 0%

commit v1 on v0

--- a/solution.py
+++ b/solution.py
@@ -50,6 +50,17 @@
 
 
 def on_device(echoes, pulse_offset, range_gates, visible):
+
+    def fill_ladders(unit, on_dim):
+        sides = jax.lax.axis_size("tile")
+        return jax.lax.all_to_all(
+            jnp.tile(unit, tuple((sides if num == on_dim else 1 for num in range(unit.ndim)))),
+            axis_name="tile",
+            split_axis=on_dim,
+            concat_axis=on_dim,
+            tiled=True,
+        )
+
     half_dev = echoes.shape[0]
     tile_dev = visible.shape[1]
     sub_count = lax.axis_size("sub")
@@ -62,7 +73,7 @@
     shown = visible.astype(jnp.float32)
     half_count = echoes.shape[0]
     norm_scale = (2.0 * PULSE_H * FREQS) ** (-0.5)
-    echo_piece = lax.all_gather(echoes, "tile", axis=1, tiled=True)
+    echo_piece = fill_ladders(echoes, on_dim=1)
     wave_piece = lax.all_gather(waves, "tile", axis=1, tiled=True)
     angle_piece = lax.all_gather(angles, "tile", axis=1, tiled=True)
     stacked = []

time: 301 us -> 277 us (0.920)
  blocking collectives: 87.4 us -> 57.9 us
    all_gather x1 -> x0, blocking collectives: 29 us -> none  [on_device(): echo_piece = lax.all_gather(echoes, 'tile', axis=1, tiled=True)]
    all_to_all x0 -> x1, starting transfers between devices: none -> 10.5 us  [fill_ladders(): jax.lax.all_to_all(jnp.tile(unit, tuple((sides if num == on_dim else 1 fo...]
    ppermute x1, starting transfers between devices: 25.8 us -> 16.7 us  [shifted(): return lax.ppermute(block, axis, route)]
  transfers between devices with their start and end apart: 2 -> 3, of which waited for: 2 -> 2; matrix products, arithmetic and copies ran while one was open for 0% -> 1% of each run, Pallas kernels for 0% -> 0%
where the time goes in v1:
time: 277 us; the launch traced here: 276 us
  waiting for transfers between devices  131 us (47%)
  blocking collectives  57.9 us (21%)
  other arithmetic  34.1 us (12%)
  starting transfers between devices  27.3 us (10%)
  between operations  14.4 us (5%)
  matrix products  7.58 us (3%)
  local copies, waits for them, and re-layouts  4.2 us (2%)
    pmax x1, waiting for transfers between devices, on_device(): full_peak = lax.pmax(local_peak, 'sub')  116 us
    all_gather x1, blocking collectives, on_device(): wave_piece = lax.all_gather(waves, 'tile', axis=1, tiled=True)  29.1 us
    all_gather x1, blocking collectives, on_device(): angle_piece = lax.all_gather(angles, 'tile', axis=1, tiled=True)  28.8 us
    ppermute x1, starting transfers between devices, shifted(): return lax.ppermute(block, axis, route)  16.7 us
    ppermute x1, waiting for transfers between devices, shifted(): return lax.ppermute(block, axis, route)  14.5 us
    another operation x2, other arithmetic  12.6 us
    all_to_all x1, starting transfers between devices, fill_ladders(): jax.lax.all_to_all(jnp.tile(unit, tuple((sides if num == on_dim else 1 fo...  10.5 us
    convert_element_type x2, other arithmetic, make_right(): imag_part = jnp.sin(phase_grid).astype(jnp.bfloat16)  8.92 us
  transfers between devices with their start and end apart: 3, of which 2 were waited for; matrix products, arithmetic and copies ran while one was open for 1% of the time, Pallas kernels for 0%

profile of v1, /device:TPU:1, one launch (start us, length us, event | category | flops | bytes accessed | tf_op | source)
XLA Modules:
  0.0 276.3 jit_solution(10889975544962052204)
XLA Ops:
  7.2 1.3 tile.10
  8.5 10.5 %all-to-all-start = ((f32[2,32,128]{2,0,1:T(2,128)}), f32[2,32,128]{2,0,1:T(2,128)S(1)}, u32[]{:S(2)}, u32[]{:S(2)}) async-start(f32[2,32,128]{2,0,1:T(2,128)} %tile.10), calls=%async_computation | async-start | bytes 65536 | tf_op jit(solution)/shard_map/all_to_all | solution.py:56
  19.0 0.0 all-reduce.2.cloned.1.call-start
  19.0 0.7 multiply_bitcast_fusion
  19.7 28.8 %all-gather = f32[32,1,2]{2,1,0:T(1,128)S(1)} all-gather(f32[1,1,2]{2,1,0:T(1,128)S(1)} %multiply_bitcast_fusion), channel_id=1, replica_groups=mesh['sub'=16,'tile'=32] {'tile'}, dimensions={0}, use_global_device_ids=true | all-gather | bytes 264 | tf_op jit(solution)/shard_map/all_gather | solution.py:78
  48.5 0.1 copy.8
  48.6 0.1 sine_bitcast_fusion.1
  48.6 0.7 multiply_add_fusion.16
  49.3 29.1 %all_gather.6 = f32[2,32,64]{2,0,1:T(2,128)S(1)} all-gather(f32[2,1,64]{2,0,1:T(2,128)S(1)} %multiply_add_fusion.16), channel_id=1, replica_groups=mesh['sub'=16,'tile'=32] {'tile'}, dimensions={1}, use_global_device_ids=true | all-gather | bytes 16896 | tf_op jit(solution)/shard_map/all_gather | solution.py:77
  78.4 0.1 slice_reduce_fusion.1
  78.6 0.1 mul.1893
  78.7 0.1 mul.1894
  78.7 0.1 mul.1900
  78.8 0.1 mul.1901
  78.9 0.1 mul.2050
  79.0 0.1 mul.2051
  79.0 0.1 mul.2054
  79.1 0.1 mul.2055
  79.2 0.1 squeeze.11
  79.2 0.1 squeeze.26
  79.3 0.7 convert_element_type.130
  80.1 0.1 fusion.122
  80.1 0.1 reshape.964
  80.2 0.1 reshape.965
  80.3 0.1 fusion.123
  80.3 0.1 reshape.966
  80.4 0.1 reshape.967
  80.5 0.1 subtract_multiply_fusion
  80.6 4.5 %sine_convert_fusion.1 = (bf16[2048,128]{1,0:T(8,128)(2,1)S(1)}, bf16[2048,128]{1,0:T(8,128)(2,1)S(1)}) fusion(f32[2048]{0:T(1024)S(1)} %get-tuple-element.117), kind=kLoop, calls=%fused_computation.125 | loop fusion | flops 786432 | bytes 1056768 | tf_op jit(solution)/shard_map/convert_element_type | solution.py:25
  85.0 4.1 %fusion.70 = bf16[2048,128]{1,0:T(8,128)(2,1)S(1)} fusion(f32[2048]{0:T(1024)S(1)} %get-tuple-element.117), kind=kLoop, calls=%fused_computation.133 | loop fusion | flops 1310720 | bytes 532480 | tf_op jit(solution)/shard_map/neg | solution.py:27
  89.1 0.1 subtract_multiply_fusion.15
  89.2 0.1 subtract_multiply_fusion.7
  89.2 0.3 add_multiply_fusion.8
  89.5 0.3 add_multiply_fusion
  89.8 4.5 %sine_convert_fusion = (bf16[2048,128]{1,0:T(8,128)(2,1)S(1)}, bf16[2048,128]{1,0:T(8,128)(2,1)S(1)}) fusion(f32[2048]{0:T(1024)S(1)} %get-tuple-element.9), kind=kLoop, calls=%fused_computation.103 | loop fusion | flops 786432 | bytes 1056768 | tf_op jit(solution)/shard_map/convert_element_type | solution.py:25
  94.2 4.1 %fusion.71 = bf16[2048,128]{1,0:T(8,128)(2,1)S(1)} fusion(f32[2048]{0:T(1024)S(1)} %get-tuple-element.9), kind=kLoop, calls=%fused_computation.134 | loop fusion | flops 1310720 | bytes 532480 | tf_op jit(solution)/shard_map/neg | solution.py:27
  98.3 6.3 %subtract_convert_fusion.8 = (bf16[128,2048]{1,0:T(8,128)(2,1)S(1)}, bf16[128,2048]{1,0:T(8,128)(2,1)S(1)}, bf16[128,2048]{1,0:T(8,128)(2,1)S(1)}, bf16[128,2048...) fusion(f32[2048]{0:T(1024)S(1)} %get-tuple-element.12, ...), kind=kLoop, calls=%fused_computation.112 | loop fusion | flops 17039360 | bytes 8527872 | tf_op jit(solution)/shard_map/convert.16
  104.6 0.5 fusion.15
  105.1 0.5 fusion.14
  105.6 0.5 fusion.13
  106.1 0.5 fusion.12
  106.5 0.5 fusion.11
  107.0 0.5 fusion.10
  107.5 0.5 fusion.9
  108.0 0.5 fusion.8
  108.5 6.3 %subtract_convert_fusion = (bf16[128,2048]{1,0:T(8,128)(2,1)S(1)}, bf16[128,2048]{1,0:T(8,128)(2,1)S(1)}, bf16[128,2048]{1,0:T(8,128)(2,1)S(1)}, bf16[128,2048]{...) fusion(f32[2048]{0:T(1024)S(1)} %get-tuple-element.29, ...), kind=kLoop, calls=%fused_computation.90 | loop fusion | flops 17039360 | bytes 8527872 | tf_op jit(solution)/shard_map/convert
  114.7 0.5 fusion.7
  115.2 0.5 fusion.6
  115.7 0.5 fusion.5
  116.2 0.5 fusion.4
  116.7 0.5 fusion.3
  117.2 0.5 fusion.2
  117.7 0.5 fusion.1
  118.2 0.4 fusion
  118.6 0.3 maximum_multiply_fusion
  118.9 0.1 fusion.120
  119.0 16.7 %collective-permute-start = (f32[8,128,256]{2,1,0:T(8,128)S(1)}, f32[8,128,256]{2,1,0:T(8,128)S(1)}, u32[]{:S(2)}, u32[]{:S(2)}) collective-permute-start(f32[8,128,256]{2,1,0:T(8,128)S(1)} %get-tuple-element.11), channel_id=1, source_target_pairs={{32,0},{64,32},{96,64},{128,96},{160,128},{192,160},{224,192},{256... | collective-permute-start | bytes 3145736 | tf_op jit(solution)/shard_map/ppermute | solution.py:18
  135.7 14.5 %collective-permute-done = f32[8,128,256]{2,1,0:T(8,128)S(1)} collective-permute-done((f32[8,128,256]{2,1,0:T(8,128)S(1)}, f32[8,128,256]{2,1,0:T(8,128)S(1)}, u32[]{:S(2)}, u32[]{:S(2)}) %collective-permute-start) | collective-permute-done | bytes 1048608 | tf_op jit(solution)/shard_map/ppermute | solution.py:18
  150.2 0.3 maximum_add_fusion
  150.6 0.0 copy-start
  150.6 1.1 fusion.17
  151.7 0.0 all-reduce.2.cloned.1.call-update
  151.7 116.4 %all-reduce.2.cloned.1.call-done = f32[8,128,128]{2,1,0:T(8,128)} async-done(((f32[8,128,128]{2,1,0:T(8,128)}), f32[8,128,128]{2,1,0:T(8,128)}) %all-reduce.2.cloned.1.call-update) | async-done | bytes 524304 | tf_op jit(solution)/shard_map/pmax | solution.py:122
  268.0 1.4 constant_dynamic-slice_fusion
  (3 shorter events, 0.0 us)
Async XLA Ops:
  8.5 71.6 %all-to-all-start = ((f32[2,32,128]{2,0,1:T(2,128)}), f32[2,32,128]{2,0,1:T(2,128)S(1)}, u32[]{:S(2)}, u32[]{:S(2)}) async-start(f32[2,32,128]{2,0,1:T(2,128)} %tile.10), calls=%async_computation | async-start | bytes 65536 | tf_op jit(solution)/shard_map/all_to_all | solution.py:56
  19.0 249.1 %all-reduce.2.cloned.1.call-start = ((), (), s32[]{:S(2)}) async-start(), calls=%async_computation.1 | async-start | bytes 1048576 | tf_op jit(solution)/shard_map/pmax | solution.py:122
  119.0 31.2 %collective-permute-start = (f32[8,128,256]{2,1,0:T(8,128)S(1)}, f32[8,128,256]{2,1,0:T(8,128)S(1)}, u32[]{:S(2)}, u32[]{:S(2)}) collective-permute-start(f32[8,128,256]{2,1,0:T(8,128)S(1)} %get-tuple-element.11), channel_id=1, source_target_pairs={{32,0},{64,32},{96,64},{128,96},{160,128},{192,160},{224,192},{256... | collective-permute-start | bytes 3145736 | tf_op jit(solution)/shard_map/ppermute | solution.py:18
  150.6 118.9 %copy-start = (f32[2,8,128,256]{3,2,1,0:T(8,128)}, f32[2,8,128,256]{3,2,1,0:T(8,128)S(1)}, u32[]{:S(2)}) copy-start(f32[2,8,128,256]{3,2,1,0:T(8,128)S(1)} %maximum_add_fusion) | copy-start | bytes 6291460
Sparse Core Ops, SparseCore 0:
  151.8 116.1 all-reduce.1
